TPU v7x, 32 devices: a whole 2x2x4 slice. The times are simulated.
32 devices in a mesh: row: 8 (over y, x, core), col: 4 (over z).
Axes of the slice: x: 2, y: 2, z: 4, core: 2. Of those that a mesh axis runs over, the one named last changes fastest.
Arguments:
- diag_factor: float32 [1024, 1024], P('row', 'col'), may hold values from -1 to 2.5, as said below
- panel_factor: float32 [4096, 1024], P('row', 'col'), may hold values from -0.09375 to 0.09375
- left_factor: float32 [4096, 2048], P('row', 'col'), may hold values from -0.09375 to 0.09375
- pivot_factor: float32 [1024, 2048], P('row', 'col'), may hold values from -0.1875 to 0.1875
- panel_adjoint: float32 [4096, 1024], P('row', 'col'), may hold values from -6 to 6
- left_adjoint: float32 [4096, 2048], P('row', 'col'), may hold values from -6 to 6
- pivot_adjoint: float32 [1024, 2048], P('row', 'col'), may hold values from -6 to 6
- diag_adjoint: float32 [1024, 1024], P('row', 'col'), may hold values from -6 to 6
Outputs:
- solved_panel: float32 [4096, 1024], P('row', 'col')
- left_out: float32 [4096, 2048], P('row', 'col')
- pivot_out: float32 [1024, 2048], P('row', 'col')
- diag_out: float32 [1024, 1024], P('row', 'col')
Inputs may be any that keep to these rules, and one draw needn't show every extreme that they name: diag_factor is lower triangular: zero above the diagonal, diagonal entries at least 1.
All inputs are finite; a program needn't handle non-finite values.
Results may differ from a plain program's by a relative error of at most 0.000073.
Values sent between devices are 32-bit elements; how exact they have to be, the bound alone decides.
No kernel may reach another device: no remote copies, remote signals or barrier semaphores. Data moves between devices by JAX's collectives and lax.ppermute only.
A program may use at most 64 MiB of HBM per device.

v0:
```python
import jax
import jax.numpy as jnp
from jax import lax
from jax.sharding import PartitionSpec as P


def right_solve(tile, source):
    return jax.scipy.linalg.solve_triangular(tile, source.T, trans="T", lower=True).T


def local(
    diag_factor,
    panel_factor,
    left_factor,
    pivot_factor,
    panel_adjoint,
    left_adjoint,
    pivot_adjoint,
    diag_adjoint,
):
    highest = lax.Precision.HIGHEST
    block_width = panel_adjoint.shape[1]
    my_col = lax.axis_index("col")
    my_row = lax.axis_index("row")
    column_block = lax.all_gather(diag_factor, "row", axis=0, tiled=True)
    whole_diag = lax.all_gather(column_block, "col", axis=1, tiled=True)
    full_rows = lax.all_gather(panel_adjoint, "col", axis=1, tiled=True)
    solved = right_solve(whole_diag, full_rows)
    solved_panel = lax.dynamic_slice_in_dim(solved, my_col * block_width, block_width, 1)
    picked = solved
    left_out = left_adjoint - jnp.dot(
        picked,
        lax.all_gather(pivot_factor, "row", axis=0, tiled=True),
        precision=highest,
        preferred_element_type=jnp.float32,
    )
    own_rows = diag_adjoint.shape[0]
    picked = solved
    square = jnp.einsum("rk,rc->kc", picked, panel_factor, precision=highest)
    pivot_part = jnp.einsum("rk,rc->kc", picked, left_factor, precision=highest)
    summed = lax.psum_scatter(
        jnp.concatenate([square, pivot_part], axis=1), "row", scatter_dimension=0, tiled=True
    )
    square_sum = summed[:, :block_width]
    pivot_sum = summed[:, block_width:]
    pivot_out = pivot_adjoint - pivot_sum
    global_row = my_row * own_rows + lax.broadcasted_iota(jnp.int32, (own_rows, block_width), 0)
    global_col = my_col * block_width + lax.broadcasted_iota(jnp.int32, (own_rows, block_width), 1)
    diag_out = diag_adjoint - jnp.where(global_col <= global_row, square_sum, 0.0)
    return (solved_panel, left_out, pivot_out, diag_out)


def solution(mesh):
    in_specs = (
        P("row", "col"),
        P("row", "col"),
        P("row", "col"),
        P("row", "col"),
        P("row", "col"),
        P("row", "col"),
        P("row", "col"),
        P("row", "col"),
    )
    out_specs = (P("row", "col"), P("row", "col"), P("row", "col"), P("row", "col"))
    return jax.shard_map(local, mesh=mesh, in_specs=in_specs, out_specs=out_specs, check_vma=False)
```

profile of v0, /device:TPU:0, one launch (start us, length us, event | category | flops | bytes accessed | tf_op | source)
XLA Modules:
  0.0 313.2 jit_solution(5399329404083906748)
XLA Ops:
  7.2 0.7 all-gather.5.cloned.1.call-update
  8.0 28.0 %all-gather.5.cloned.1.call-done = f32[1024,256]{1,0:T(8,128)} async-done(((f32[128,256]{1,0:T(8,128)}), f32[1024,256]{1,0:T(8,128)}) %all-gather.5.cloned.1.call-update) | async-done | bytes 1048592 | tf_op jit(solution)/shard_map/all_gather | solution.py:25
  36.1 0.7 all-gather.9.cloned.1.call-update
  36.8 0.5 all-gather.11.cloned.1.call-update
  37.4 80.9 %all-gather.7.cloned.1.call-done = f32[1024,1024]{1,0:T(8,128)} async-done(((f32[1024,256]{1,0:T(8,128)}), f32[1024,1024]{1,0:T(8,128)}) %all-gather.7.cloned.1.call-update) | async-done | bytes 4194320 | tf_op jit(solution)/shard_map/all_gather | solution.py:26
  118.3 4.8 %fusion = f32[1024,1024]{1,0:T(8,128)} fusion(f32[1024,1024]{1,0:T(8,128)} %all-gather.7.cloned.1.call-done), kind=kLoop, calls=%fused_computation.3 | loop fusion | flops 2097152 | bytes 8388608 | tf_op jit(solution)/shard_map/jit(_solve_triangular)/triangular_solve | solution.py:8
  123.1 23.2 %while.1 = (s32[]{:T(128)}, f32[1024,1024]{1,0:T(8,128)}, s32[8,2]{0,1:T(2,128)S(1)}, f32[8,128,128]{2,1,0:T(8,128)S(1)}, s32[]{:T(128)}) while((s32[]{:T(128)}, f32[1024,1024]{1,0:T(8,128)}, s32[8,2]{0,1:T(2,128)S(1)}, f32[8,128,128]{2,1,0:T(8,128)S(1)}, s32[]{:T(128)}) %tuple.27), condition=%wide.while_cond, body=%wide.while_body.sunk | while | flops 2 | bytes 131181 | solution.py:8
  123.2 0.5 fusion.56
  123.7 2.3 bitcast_dynamic-update-slice_fusion.2
  126.1 0.5 fusion.56
  126.6 2.3 bitcast_dynamic-update-slice_fusion.2
  129.0 0.5 fusion.56
  129.5 2.3 bitcast_dynamic-update-slice_fusion.2
  131.9 0.5 fusion.56
  132.4 2.3 bitcast_dynamic-update-slice_fusion.2
  134.8 0.5 fusion.56
  135.3 2.3 bitcast_dynamic-update-slice_fusion.2
  137.7 0.5 fusion.56
  138.3 2.3 bitcast_dynamic-update-slice_fusion.2
  140.6 0.5 fusion.56
  141.2 2.3 bitcast_dynamic-update-slice_fusion.2
  143.6 0.5 fusion.56
  144.1 2.2 bitcast_dynamic-update-slice_fusion.2
  146.3 78.8 %custom-call.4 = f32[8,128,128]{1,2,0:T(8,128)S(1)} custom-call(f32[8,128,128]{2,1,0:T(8,128)S(1)} %get-tuple-element.11), custom_call_target="InvertDiagBlocksLowerTriangular" | custom-call | tf_op jit(solution)/shard_map/jit(_solve_triangular)/triangular_solve | solution.py:8
  225.2 1.5 fusion.19
  226.7 1.6 convolution_subtract_fusion.4
  228.7 2.0 convolution_subtract_fusion.3
  231.1 2.4 convolution_subtract_fusion.6
  233.5 0.4 fusion.28
  233.9 2.8 convolution_subtract_fusion.7
  237.1 3.2 %convolution_subtract_fusion.2 = f32[128,512]{0,1:T(8,128)S(1)} fusion(f32[640,512]{1,0:T(8,128)S(1)} %constant_dynamic-update-slice_fusion, f32[1024,1024]{1,0:T(8,128)} %get-tuple-element.83, f32[1024,512]{0,1:T(8,128)S(1)} %bitcast.65), kind=kOutput, calls=%fused_computation.8 | convolution fusion | flops 503382016 | bytes 2162688 | tf_op jit(solution)/shard_map/jit(_solve_triangular)/triangular_solve | solution.py:8
  240.3 0.4 constant_dynamic-update-slice_fusion.10
  240.9 3.6 %convolution_subtract_fusion.5 = f32[128,512]{0,1:T(8,128)S(1)} fusion(f32[768,512]{1,0:T(8,128)S(1)} %constant_dynamic-update-slice_fusion.5, f32[1024,1024]{1,0:T(8,128)} %get-tuple-element.83, f32[1024,512]{0,1:T(8,128)S(1)} %bitcast.66), kind=kOutput, calls=%fused_computation.11 | convolution fusion | flops 604045312 | bytes 2490368 | tf_op jit(solution)/shard_map/jit(_solve_triangular)/triangular_solve | solution.py:8
  245.0 4.3 %convolution_subtract_fusion.1 = f32[128,512]{0,1:T(8,128)S(1)} fusion(f32[896,512]{1,0:T(8,128)S(1)} %constant_dynamic-update-slice_fusion.11, f32[1024,1024]{1,0:T(8,128)} %get-tuple-element.83, f32[1024,512]{0,1:T(8,128)S(1)} %bitcast.67), kind=kOutput, calls=%fused_computation.7 | convolution fusion | flops 704708608 | bytes 2818048 | tf_op jit(solution)/shard_map/jit(_solve_triangular)/triangular_solve | solution.py:8
  249.4 1.3 convolution_dynamic-update-slice_fusion
  250.8 2.0 fusion.36
  252.9 3.5 %fusion.37 = f32[1024,512]{0,1:T(8,128)S(1)} fusion(f32[1024,512]{1,0:T(8,128)S(1)} %constant_dynamic-update-slice_fusion.18, f32[512,512]{1,0:T(8,128)S(1)} %copy-done), kind=kOutput, calls=%fused_computation.89 | convolution fusion | flops 3221225472 | bytes 5242880 | tf_op jit(solution)/shard_map/rk,rc->kc/dot_general | solution.py:40
  256.4 2.0 pad_maximum_fusion
  258.5 1.1 copy.12
  259.5 1.0 copy.13
  260.6 0.8 dynamic-slice_bitcast_fusion
  261.4 2.1 copy.14
  263.5 6.6 %convolution_subtract_fusion = f32[512,512]{1,0:T(8,128)} fusion(f32[512,512]{1,0:T(8,128)} %param.13, f32[1024,512]{1,0:T(8,128)S(1)} %constant_dynamic-update-slice_fusion.18, f32[1024,512]{1,0:T(8,128)} %all-gather.11.cloned.1.call-done), kind=kOutput, calls=%fused_computation.5 | convolution fusion | flops 3221487616 | bytes 6291456 | tf_op jit(solution)/shard_map/dot_general | solution.py:31
  270.1 33.0 %reduce-scatter.2.cloned.1.call-done = f32[128,768]{0,1:T(8,128)} async-done(((f32[1024,768]{0,1:T(8,128)}), f32[128,768]{0,1:T(8,128)}) %reduce-scatter.2.cloned.1.call-update) | async-done | bytes 393232 | tf_op jit(solution)/shard_map/reduce_scatter | solution.py:41
  303.1 1.0 slice_subtract_fusion
  304.1 0.8 copy.15
  304.9 1.0 fusion.23
  305.9 0.8 copy.16
  (56 shorter events, 2.8 us)
Async XLA Ops:
  7.2 245.7 %copy-start = (f32[512,512]{1,0:T(8,128)S(1)}, f32[512,512]{1,0:T(8,128)}, u32[]{:S(2)}) copy-start(f32[512,512]{1,0:T(8,128)} %param.10) | copy-start | bytes 3145732
  7.2 28.8 %all-gather.5.cloned.1.call-start = ((), (), s32[]{:S(2)}) async-start(), calls=%async_computation.1 | async-start | bytes 1179648 | tf_op jit(solution)/shard_map/all_gather | solution.py:25
  7.9 110.4 %all-gather.7.cloned.1.call-start = ((), (), s32[]{:S(2)}) async-start(), calls=%async_computation.2 | async-start | bytes 5242880 | tf_op jit(solution)/shard_map/all_gather | solution.py:26
  36.0 189.1 %all-gather.9.cloned.1.call-start = ((), (), s32[]{:S(2)}) async-start(), calls=%async_computation.3 | async-start | bytes 2621440 | tf_op jit(solution)/shard_map/all_gather | solution.py:27
  36.8 226.7 %all-gather.11.cloned.1.call-start = ((), (), s32[]{:S(2)}) async-start(), calls=%async_computation.4 | async-start | bytes 2359296 | tf_op jit(solution)/shard_map/all_gather | solution.py:33
  37.3 265.8 %reduce-scatter.2.cloned.1.call-start = ((), (), s32[]{:S(2)}) async-start(), calls=%async_computation.5 | async-start | bytes 3538944 | tf_op jit(solution)/shard_map/reduce_scatter | solution.py:41
  225.1 19.4 %copy-start.3 = (f32[8,128,128]{1,2,0:T(8,128)}, f32[8,128,128]{1,2,0:T(8,128)S(1)}, u32[]{:S(2)}) copy-start(f32[8,128,128]{1,2,0:T(8,128)S(1)} %custom-call.4) | copy-start | bytes 1572868
  225.1 5.9 %copy-start.1 = (f32[512,1024]{1,0:T(8,128)S(1)}, f32[512,1024]{1,0:T(8,128)}, u32[]{:S(2)}) copy-start(f32[512,1024]{1,0:T(8,128)} %all-gather.9.cloned.1.call-done) | copy-start | bytes 6291460
  249.4 1.5 copy-start.2
Sparse Core Ops, SparseCore 0:
  9.9 26.0 all-gather.4
  37.6 80.7 all-gather.6
  119.9 44.1 all-gather.8
  165.9 26.7 all-gather.10
  258.6 44.4 reduce-scatter.1
where the time goes:
time: 314 us; the launch traced here: 313 us
  waiting for transfers between devices  144 us (46%)
  other arithmetic  87.5 us (28%)
  matrix products  37.1 us (12%)
  local copies, waits for them, and re-layouts  30.1 us (10%)
  between operations  14.2 us (5%)
    another operation x3, other arithmetic, right_solve(): jax.scipy.linalg.solve_triangular(tile, source.T, trans='T', lower=True)  83.5 us
    all_gather x1, waiting for transfers between devices, local(): whole_diag = lax.all_gather(column_block, 'col', axis=1, tiled=True)  80.9 us
    reduce_scatter x1, waiting for transfers between devices, local(): lax.psum_scatter(jnp.concatenate([square, pivot_part], axis=1), 'row', sc...  33 us
    all_gather x1, waiting for transfers between devices, local(): column_block = lax.all_gather(diag_factor, 'row', axis=0, tiled=True)  28 us
    another operation x15, matrix products, right_solve(): jax.scipy.linalg.solve_triangular(tile, source.T, trans='T', lower=True)  24.9 us
    another operation x24, local copies, waits for them, and re-layouts  23.1 us
    dot_general x1, matrix products, local(): jnp.dot(picked, lax.all_gather(pivot_factor, 'row', axis=0, tiled=True),...  6.61 us
  transfers between devices with their start and end apart: 5, of which 3 were waited for; matrix products, arithmetic and copies ran while one was open for 48% of the time, Pallas kernels for 0%

commit v1 on v0

--- a/solution.py
+++ b/solution.py
@@ -23,8 +23,18 @@
     my_col = lax.axis_index("col")
     my_row = lax.axis_index("row")
     column_block = lax.all_gather(diag_factor, "row", axis=0, tiled=True)
-    whole_diag = lax.all_gather(column_block, "col", axis=1, tiled=True)
-    full_rows = lax.all_gather(panel_adjoint, "col", axis=1, tiled=True)
+
+    def _draw_pipes(x_part, mat):
+        h_now = jnp.split(
+            lax.all_gather(
+                jnp.concatenate([x_part, mat], axis=0), axis=1, tiled=True, axis_name="col"
+            ),
+            [x_part.shape[0]],
+            axis=0,
+        )
+        return h_now
+
+    whole_diag, full_rows = _draw_pipes(column_block, mat=panel_adjoint)
     solved = right_solve(whole_diag, full_rows)
     solved_panel = lax.dynamic_slice_in_dim(solved, my_col * block_width, block_width, 1)
     picked = solved

time: 314 us -> 350 us (1.11)
  waiting for transfers between devices: 144 us -> 177 us
    all_gather x2 -> x1, waiting for transfers between devices: 81 us -> 115 us  [_draw_pipes(): lax.all_gather(jnp.concatenate([x_part, mat], axis=0), axis=1, tiled=True...]
  transfers between devices with their start and end apart: 5 -> 4, of which waited for: 3 -> 3; matrix products, arithmetic and copies ran while one was open for 48% -> 43% of each run, Pallas kernels for 0% -> 0%
where the time goes in v1:
time: 350 us; the launch traced here: 349 us
  waiting for transfers between devices  177 us (51%)
  other arithmetic  90.2 us (26%)
  matrix products  35.5 us (10%)
  local copies, waits for them, and re-layouts  32.3 us (9%)
  between operations  14.2 us (4%)
    all_gather x1, waiting for transfers between devices, _draw_pipes(): lax.all_gather(jnp.concatenate([x_part, mat], axis=0), axis=1, tiled=True...  115 us
    another operation x3, other arithmetic, right_solve(): jax.scipy.linalg.solve_triangular(tile, source.T, trans='T', lower=True)  83.6 us
    reduce_scatter x1, waiting for transfers between devices, local(): lax.psum_scatter(jnp.concatenate([square, pivot_part], axis=1), 'row', sc...  32.7 us
    all_gather x1, waiting for transfers between devices, local(): column_block = lax.all_gather(diag_factor, 'row', axis=0, tiled=True)  28 us
    another operation x15, matrix products, right_solve(): jax.scipy.linalg.solve_triangular(tile, source.T, trans='T', lower=True)  23.4 us
    another operation x24, local copies, waits for them, and re-layouts  23.1 us
  transfers between devices with their start and end apart: 4, of which 3 were waited for; matrix products, arithmetic and copies ran while one was open for 43% of the time, Pallas kernels for 0%

profile of v1, /device:TPU:0, one launch (start us, length us, event | category | flops | bytes accessed | tf_op | source)
XLA Modules:
  0.0 349.4 jit_solution(1746635386249456011)
XLA Ops:
  7.2 0.7 all-gather.4.cloned.1.call-update
  8.0 28.0 %all-gather.4.cloned.1.call-done = f32[1024,256]{1,0:T(8,128)} async-done(((f32[128,256]{1,0:T(8,128)}), f32[1024,256]{1,0:T(8,128)}) %all-gather.4.cloned.1.call-update) | async-done | bytes 1048592 | tf_op jit(solution)/shard_map/all_gather | solution.py:25
  36.0 2.6 pad_maximum_fusion.1
  38.7 0.7 all-gather.8.cloned.1.call-update
  39.5 114.7 %all-gather.6.cloned.1.call-done = f32[1536,1024]{1,0:T(8,128)} async-done(((f32[1536,256]{1,0:T(8,128)}), f32[1536,1024]{1,0:T(8,128)}) %all-gather.6.cloned.1.call-update) | async-done | bytes 6291472 | tf_op jit(solution)/shard_map/all_gather | solution.py:29
  154.1 4.8 %slice_select_fusion = f32[1024,1024]{1,0:T(8,128)} fusion(f32[1536,1024]{1,0:T(8,128)} %all-gather.6.cloned.1.call-done), kind=kLoop, calls=%fused_computation.2 | loop fusion | flops 2097152 | bytes 8388608 | tf_op jit(solution)/shard_map/jit(_solve_triangular)/triangular_solve | solution.py:8
  158.9 23.2 %while.1 = (s32[]{:T(128)}, f32[1024,1024]{1,0:T(8,128)}, s32[8,2]{0,1:T(2,128)S(1)}, f32[8,128,128]{2,1,0:T(8,128)S(1)}, s32[]{:T(128)}) while((s32[]{:T(128)}, f32[1024,1024]{1,0:T(8,128)}, s32[8,2]{0,1:T(2,128)S(1)}, f32[8,128,128]{2,1,0:T(8,128)S(1)}, s32[]{:T(128)}) %tuple.27), condition=%wide.while_cond, body=%wide.while_body.sunk | while | flops 2 | bytes 131189 | solution.py:8
  159.0 0.5 fusion.55
  159.5 2.3 bitcast_dynamic-update-slice_fusion.2
  161.9 0.5 fusion.55
  162.5 2.3 bitcast_dynamic-update-slice_fusion.2
  164.8 0.5 fusion.55
  165.4 2.3 bitcast_dynamic-update-slice_fusion.2
  167.7 0.5 fusion.55
  168.3 2.3 bitcast_dynamic-update-slice_fusion.2
  170.7 0.5 fusion.55
  171.2 2.3 bitcast_dynamic-update-slice_fusion.2
  173.6 0.5 fusion.55
  174.1 2.3 bitcast_dynamic-update-slice_fusion.2
  176.5 0.5 fusion.55
  177.0 2.3 bitcast_dynamic-update-slice_fusion.2
  179.4 0.5 fusion.55
  179.9 2.2 bitcast_dynamic-update-slice_fusion.2
  182.2 78.8 %custom-call.4 = f32[8,128,128]{1,2,0:T(8,128)S(1)} custom-call(f32[8,128,128]{2,1,0:T(8,128)S(1)} %get-tuple-element.11), custom_call_target="InvertDiagBlocksLowerTriangular" | custom-call | tf_op jit(solution)/shard_map/jit(_solve_triangular)/triangular_solve | solution.py:8
  261.0 1.9 slice_bitcast_fusion
  262.9 0.4 fusion.18
  263.3 1.4 convolution_subtract_fusion.4
  265.1 1.9 convolution_subtract_fusion.3
  267.4 2.4 convolution_subtract_fusion.6
  269.8 0.4 fusion.27
  270.2 2.8 convolution_subtract_fusion.7
  273.4 3.2 convolution_subtract_fusion.2
  277.2 3.6 %convolution_subtract_fusion.5 = f32[128,512]{0,1:T(8,128)S(1)} fusion(f32[768,512]{1,0:T(8,128)S(1)} %constant_dynamic-update-slice_fusion.5, f32[1024,1024]{1,0:T(8,128)} %get-tuple-element.82, f32[1024,512]{0,1:T(8,128)S(1)} %slice_bitcast_fusion), kind=kOutput, calls=%fused_computation.13 | convolution fusion | flops 604045312 | bytes 2490368 | tf_op jit(solution)/shard_map/jit(_solve_triangular)/triangular_solve | solution.py:8
  281.6 4.2 %convolution_subtract_fusion.1 = f32[128,512]{0,1:T(8,128)S(1)} fusion(f32[896,512]{1,0:T(8,128)S(1)} %constant_dynamic-update-slice_fusion.11, f32[1024,1024]{1,0:T(8,128)} %get-tuple-element.82, f32[1024,512]{0,1:T(8,128)S(1)} %slice_bitcast_fusion), kind=kOutput, calls=%fused_computation.9 | convolution fusion | flops 704708608 | bytes 2818048 | tf_op jit(solution)/shard_map/jit(_solve_triangular)/triangular_solve | solution.py:8
  285.8 1.3 convolution_dynamic-update-slice_fusion
  287.2 2.0 fusion.35
  289.3 3.5 %fusion.36 = f32[1024,512]{0,1:T(8,128)S(1)} fusion(f32[1024,512]{1,0:T(8,128)S(1)} %constant_dynamic-update-slice_fusion.18, f32[512,512]{1,0:T(8,128)S(1)} %copy-done), kind=kOutput, calls=%fused_computation.91 | convolution fusion | flops 3221225472 | bytes 5242880 | tf_op jit(solution)/shard_map/rk,rc->kc/dot_general | solution.py:50
  292.8 2.0 pad_maximum_fusion
  294.9 1.1 copy.12
  296.0 1.0 copy.13
  297.0 0.8 dynamic-slice_bitcast_fusion
  297.8 2.1 copy.14
  300.0 6.6 %convolution_subtract_fusion = f32[512,512]{1,0:T(8,128)} fusion(f32[512,512]{1,0:T(8,128)} %param.13, f32[1024,512]{1,0:T(8,128)S(1)} %constant_dynamic-update-slice_fusion.18, f32[1024,512]{1,0:T(8,128)} %all-gather.8.cloned.1.call-done), kind=kOutput, calls=%fused_computation.7 | convolution fusion | flops 3221487616 | bytes 6291456 | tf_op jit(solution)/shard_map/dot_general | solution.py:41
  306.5 32.7 %reduce-scatter.2.cloned.1.call-done = f32[128,768]{0,1:T(8,128)} async-done(((f32[1024,768]{0,1:T(8,128)}), f32[128,768]{0,1:T(8,128)}) %reduce-scatter.2.cloned.1.call-update) | async-done | bytes 393232 | tf_op jit(solution)/shard_map/reduce_scatter | solution.py:51
  339.2 1.0 slice_subtract_fusion
  340.2 0.8 copy.15
  341.1 1.0 fusion.22
  342.1 0.8 copy.16
  (53 shorter events, 3.3 us)
Async XLA Ops:
  7.2 282.1 %copy-start = (f32[512,512]{1,0:T(8,128)S(1)}, f32[512,512]{1,0:T(8,128)}, u32[]{:S(2)}) copy-start(f32[512,512]{1,0:T(8,128)} %param.10) | copy-start | bytes 3145732
  7.2 28.8 %all-gather.4.cloned.1.call-start = ((), (), s32[]{:S(2)}) async-start(), calls=%async_computation.1 | async-start | bytes 1179648 | tf_op jit(solution)/shard_map/all_gather | solution.py:25
  7.9 146.2 %all-gather.6.cloned.1.call-start = ((), (), s32[]{:S(2)}) async-start(), calls=%async_computation.2 | async-start | bytes 7864320 | tf_op jit(solution)/shard_map/all_gather | solution.py:29
  38.7 261.3 %all-gather.8.cloned.1.call-start = ((), (), s32[]{:S(2)}) async-start(), calls=%async_computation.3 | async-start | bytes 2359296 | tf_op jit(solution)/shard_map/all_gather | solution.py:43
  39.4 299.8 %reduce-scatter.2.cloned.1.call-start = ((), (), s32[]{:S(2)}) async-start(), calls=%async_computation.4 | async-start | bytes 3538944 | tf_op jit(solution)/shard_map/reduce_scatter | solution.py:51
  261.0 19.8 %copy-start.2 = (f32[8,128,128]{1,2,0:T(8,128)}, f32[8,128,128]{1,2,0:T(8,128)S(1)}, u32[]{:S(2)}) copy-start(f32[8,128,128]{1,2,0:T(8,128)S(1)} %custom-call.4) | copy-start | bytes 1572868
  285.8 1.5 copy-start.1
Sparse Core Ops, SparseCore 0:
  9.9 26.0 all-gather.3
  38.8 115.3 all-gather.5
  156.0 25.9 all-gather.7
  295.0 44.2 reduce-scatter.1
